TPU v7x, 512 devices: a whole 4x8x8 slice. The times are simulated.
512 devices in a mesh: sx: 32 (over y_lo, z), sy: 16 (over y_hi, x, core).
Axes of the slice: x: 4, y: 8 (y_hi: 2, y_lo: 4; y = y_hi * 4 + y_lo), z: 8, core: 2. Of those that a mesh axis runs over, the one named last changes fastest.
Arguments:
- right_vectors: bfloat16 [32, 1024, 4096], P(None, 'sx', 'sy'), may hold values from -6 to 6
- left_vectors: bfloat16 [64, 1024, 4096], P(None, 'sx', 'sy'), may hold values from -6 to 6
- classes: int32 [1024, 4096], P('sx', 'sy'), may hold values from 0 to 3
- class_energy: float32 [4], replicated, may hold values from -1.5 to 1.5
- bond_mask_grid: int32 [2, 1024, 4096], P(None, 'sx', 'sy'), may hold values 0 or 1
- order: int32 [5], replicated, may hold values from 0 to 4, each once
Outputs:
- gamma: float32 [5, 64, 32], P(None, 'sy')
Inputs may be any that keep to these rules, and one draw needn't show every extreme that they name: Each order from 0 to 4 appears once.
All inputs are finite; a program needn't handle non-finite values. No bound on the sum of `bond_mask_grid` on one device may be relied on, other than what follows from the above.
Results may differ from a plain program's by a relative error of at most 0.0003.
Values sent between devices are 32-bit elements; how exact they have to be, the bound alone decides.
No kernel may reach another device: no remote copies, remote signals or barrier semaphores. Data moves between devices by JAX's collectives and lax.ppermute only.
A program may use at most 64 MiB of HBM per device.

v0:
```python
import jax
import jax.numpy as jnp
from jax import lax
from jax.sharding import PartitionSpec as P

MOMENTS = 5
half_root = 0.8660254037844386
spectral_scale = 4.6


def shifted(value, axis, by):
    length = lax.axis_size(axis)
    return lax.ppermute(value, axis, [(i, (i + by) % length) for i in range(length)])


def with_halo(value, sides, width):
    for axis, dim in sides:
        size, length = (lax.axis_size(axis), value.shape[dim])
        up = [(i, (i + 1) % size) for i in range(size)]
        down = [(j, i) for i, j in up]
        last = lax.slice_in_dim(value, length - width, length, axis=dim)
        initial = lax.slice_in_dim(value, 0, width, axis=dim)
        before = lax.ppermute(last, axis, up)
        after = lax.ppermute(initial, axis, down)
        value = jnp.concatenate([before, value, after], axis=dim)
    return value


def offsets(padded):
    return (padded[:, 2:, 1:-1], padded[:, :-2, 1:-1], padded[:, 1:-1, 2:], padded[:, 1:-1, :-2])


def shards(right_vectors, left_vectors, classes, class_energy, bond_mask_grid, order):
    rows_x, rows_y = classes.shape
    west_row = shifted(bond_mask_grid[0, -1:, :], "sx", 1)
    south_column = shifted(bond_mask_grid[1, :, -1:], "sy", 1)
    hmask = bond_mask_grid[0].astype(jnp.float32)
    vertical_mask = bond_mask_grid[1].astype(jnp.float32)
    west_mask = jnp.concatenate([west_row.astype(jnp.float32), hmask[:-1]], axis=0)
    south_mask = jnp.concatenate([south_column.astype(jnp.float32), vertical_mask[:, :-1]], axis=1)
    xpos = jnp.arange(rows_x, dtype=jnp.int32)[:, None]
    ypos = jnp.arange(rows_y, dtype=jnp.int32)[None, :]
    sublattice_first = ((xpos + ypos) % 2 == 0).astype(jnp.float32)
    sublattice_second = 1.0 - sublattice_first
    sign = sublattice_first - sublattice_second
    upper_neighbour = vertical_mask * sublattice_first
    lower_neighbour = south_mask * sublattice_second
    energy = jnp.zeros((rows_x, rows_y), jnp.float32)
    for level in range(class_energy.shape[0]):
        energy = energy + (classes == level).astype(jnp.float32) * class_energy[level]

    def beside_all(field):
        return offsets(with_halo(field, (("sx", 1), ("sy", 2)), 1))

    nleft = left_vectors.shape[0]
    nright = right_vectors.shape[0]
    cells = rows_x * rows_y
    left_field = left_vectors.astype(jnp.float32)
    left_flat = left_field.reshape(nleft, cells)
    count = MOMENTS
    moments = []
    u_prev = None
    pe, pw, pn, ps = beside_all(right_vectors.astype(jnp.float32))
    u_now = 0.5 * sign * (hmask * pe + west_mask * pw) - upper_neighbour * pn + lower_neighbour * ps
    for step in range(count):
        final = step == count - 1
        parts = None
        parts = beside_all(u_now)
        vel_pe, vel_pw, vel_pn, vel_ps = parts
        moved = (-half_root * (hmask * vel_pe - west_mask * vel_pw)).reshape(nright, cells)
        moments.append(
            jnp.dot(
                left_flat,
                moved.T,
                precision=lax.Precision.HIGHEST,
                preferred_element_type=jnp.float32,
            )
        )
        if not final:
            hamilton_pe, hamilton_pw, hamilton_pn, hamilton_ps = parts
            image = (
                energy * u_now
                - hmask * hamilton_pe
                - west_mask * hamilton_pw
                - upper_neighbour * hamilton_pn
                - lower_neighbour * hamilton_ps
            ) / spectral_scale
            if step == 0:
                u_next = image
            else:
                u_next = 2.0 * image - u_prev
            u_prev, u_now = (u_now, u_next)
    partial_tiles = jnp.stack(moments)
    owned = nleft // lax.axis_size("sy")
    total = lax.psum(partial_tiles, ("sx", "sy"))
    mine = lax.dynamic_slice_in_dim(total, lax.axis_index("sy") * owned, owned, 1)
    all_sites = cells * lax.axis_size("sx") * lax.axis_size("sy")
    mine = mine * (1.0 / jnp.sqrt(jnp.float32(all_sites)))
    select = (order[:, None] == jnp.arange(count, dtype=jnp.int32)[None, :]).astype(jnp.float32)
    return jnp.einsum("sm,mlr->slr", select, mine, precision=lax.Precision.HIGHEST)


def solution(mesh):
    in_specs = (
        P(None, "sx", "sy"),
        P(None, "sx", "sy"),
        P("sx", "sy"),
        P(),
        P(None, "sx", "sy"),
        P(),
    )
    out_specs = P(None, "sy", None)
    return jax.shard_map(shards, mesh=mesh, in_specs=in_specs, out_specs=out_specs, check_vma=False)
```

profile of v0, /device:TPU:1, one launch (start us, length us, event | category | flops | bytes accessed | tf_op | source)
XLA Modules:
  0.0 309.3 jit_solution(4009982580344775790)
XLA Ops:
  1.5 14.5 %collective-permute-start = (f32[32,1,256]{2,0,1:T(8,128)S(1)}, f32[32,1,256]{2,0,1:T(8,128)S(1)}, u32[]{:S(2)}, u32[]{:S(2)}) collective-permute-start(f32[32,1,256]{2,0,1:T(8,128)S(1)} %get-tuple-element.30), channel_id=1, source_target_pairs={{16,0},{32,16},{48,32},{64,48},{80,64},{96,80},{112,96},{128,112},... | collective-permute-start | bytes 98312 | tf_op jit(solution)/shard_map/ppermute | solution.py:24
  18.1 4.0 %collective-permute-start.4 = (s32[32,1]{0,1:T(1,128)S(1)}, s32[32,1]{0,1:T(1,128)S(1)}, u32[]{:S(2)}, u32[]{:S(2)}) collective-permute-start(s32[32,1]{0,1:T(1,128)S(1)} %bitcast.60), channel_id=1, source_target_pairs={{0,1},{1,2},{2,3},{3,4},{4,5},{5,6},{6,7},{7,8},{8,9},{9,10},{10,1... | collective-permute-start | bytes 392 | tf_op jit(solution)/shard_map/ppermute | solution.py:13
  24.3 6.3 %collective-permute-done.1 = s32[1,256]{1,0:T(1,128)S(1)} collective-permute-done((s32[1,256]{1,0:T(1,128)S(1)}, s32[1,256]{1,0:T(1,128)S(1)}, u32[]{:S(2)}, u32[]{:S(2)}) %collective-permute-start.1) | collective-permute-done | bytes 1056 | tf_op jit(solution)/shard_map/ppermute | solution.py:13
  31.4 2.8 collective-permute-start.5
  43.3 4.2 %collective-permute-start.6 = (f32[32,1,256]{2,0,1:T(8,128)S(1)}, f32[32,1,256]{2,0,1:T(8,128)S(1)}, u32[]{:S(2)}, u32[]{:S(2)}) collective-permute-start(f32[32,1,256]{2,0,1:T(8,128)S(1)} %get-tuple-element.28), channel_id=1, source_target_pairs={{16,0},{32,16},{48,32},{64,48},{80,64},{96,80},{112,96},{128,112},... | collective-permute-start | bytes 98312 | tf_op jit(solution)/shard_map/ppermute | solution.py:24
  50.1 6.0 %collective-permute-done.7 = f32[32,1,256]{2,0,1:T(8,128)S(1)} collective-permute-done((f32[32,1,256]{2,0,1:T(8,128)S(1)}, f32[32,1,256]{2,0,1:T(8,128)S(1)}, u32[]{:S(2)}, u32[]{:S(2)}) %collective-permute-start.7) | collective-permute-done | bytes 32800 | tf_op jit(solution)/shard_map/ppermute | solution.py:23
  58.8 2.5 collective-permute-start.9
  62.7 10.5 %collective-permute-start.8 = (f32[32,34,1]{1,0,2:T(8,128)S(1)}, f32[32,34,1]{1,0,2:T(8,128)}, u32[]{:S(2)}, u32[]{:S(2)}) collective-permute-start(f32[32,34,1]{1,0,2:T(8,128)S(1)} %copy.129), channel_id=1, source_target_pairs={{1,0},{2,1},{3,2},{4,3},{5,4},{6,5},{7,6},{8,7},{9,8},{10,9},{11,1... | collective-permute-start | bytes 13064 | tf_op jit(solution)/shard_map/ppermute | solution.py:24
  73.2 3.2 %broadcast_multiply_fusion.1 = (f32[32,256]{1,0:T(8,128)}, f32[32,256]{1,0:T(8,128)S(1)}) fusion(f32[]{:T(128)} %bitcast.12, s32[32,256]{1,0:T(8,128)S(1)} %copy-done.25, f32[]{:T(128)} %bitcast.11, f32[]{:T(128)} %bitcast.10, f32[]{:T(128)} %bitcast.9), kind=kLoop, calls=%fused_computation.158 | loop fusion | flops 98304 | bytes 98320 | tf_op jit(solution)/shard_map/mul | solution.py:82
  77.8 2.1 copy.92
  79.9 2.9 broadcast_multiply_fusion
  84.8 3.4 %collective-permute-start.11 = (f32[32,1,256]{2,0,1:T(8,128)S(1)}, f32[32,1,256]{2,0,1:T(8,128)S(1)}, u32[]{:S(2)}, u32[]{:S(2)}) collective-permute-start(f32[32,1,256]{2,0,1:T(8,128)S(1)} %get-tuple-element.25), channel_id=1, source_target_pairs={{0,16},{16,32},{32,48},{48,64},{64,80},{80,96},{96,112},{112,128},... | collective-permute-start | bytes 98312 | tf_op jit(solution)/shard_map/ppermute | solution.py:23
  88.2 5.2 %collective-permute-done.11 = f32[32,1,256]{2,0,1:T(8,128)S(1)} collective-permute-done((f32[32,1,256]{2,0,1:T(8,128)S(1)}, f32[32,1,256]{2,0,1:T(8,128)S(1)}, u32[]{:S(2)}, u32[]{:S(2)}) %collective-permute-start.11) | collective-permute-done | bytes 32800 | tf_op jit(solution)/shard_map/ppermute | solution.py:23
  96.6 10.8 %collective-permute-start.12 = (f32[32,34,1]{1,0,2:T(8,128)S(1)}, f32[32,34,1]{1,0,2:T(8,128)S(1)}, u32[]{:S(2)}, u32[]{:S(2)}) collective-permute-start(f32[32,34,1]{1,0,2:T(8,128)S(1)} %copy.131), channel_id=1, source_target_pairs={{1,0},{2,1},{3,2},{4,3},{5,4},{6,5},{7,6},{8,7},{9,8},{10,9},{11,1... | collective-permute-start | bytes 13064 | tf_op jit(solution)/shard_map/ppermute | solution.py:24
  110.1 5.8 %fusion.32 = f32[32,32,256]{2,0,1:T(8,128)S(1)} fusion(f32[32,34,1]{2,0,1:T(8,128)} %copy.100, f32[32,1,256]{2,0,1:T(8,128)S(1)} %collective-permute-done.10, f32[32,32,256]{2,0,1:T(8,128)} %copy-done.1, f32[32,1,256]{2,0,1:T(8,128)S(1)} %collective-permute-done.11, f32[32,34,1]{2,0,1:T(8,128)} %copy.98, f32[32,32,256]{2,0,1:T(8,128)} %get-tuple-element.8, ...), kind=kLoop, calls=%fused_computation.59 | loop fusion | flops 9175040 | bytes 4539392 | tf_op jit(solution)/shard_map/sub | solution.py:91
  117.8 3.4 %collective-permute-start.15 = (f32[32,1,256]{2,0,1:T(8,128)S(1)}, f32[32,1,256]{2,0,1:T(8,128)S(1)}, u32[]{:S(2)}, u32[]{:S(2)}) collective-permute-start(f32[32,1,256]{2,0,1:T(8,128)S(1)} %get-tuple-element.23), channel_id=1, source_target_pairs={{0,16},{16,32},{32,48},{48,64},{64,80},{80,96},{96,112},{112,128},... | collective-permute-start | bytes 98312 | tf_op jit(solution)/shard_map/ppermute | solution.py:23
  121.2 5.2 %collective-permute-done.15 = f32[32,1,256]{2,0,1:T(8,128)S(1)} collective-permute-done((f32[32,1,256]{2,0,1:T(8,128)S(1)}, f32[32,1,256]{2,0,1:T(8,128)S(1)}, u32[]{:S(2)}, u32[]{:S(2)}) %collective-permute-start.15) | collective-permute-done | bytes 32800 | tf_op jit(solution)/shard_map/ppermute | solution.py:23
  133.7 11.0 %collective-permute-start.16 = (f32[32,34,1]{1,0,2:T(8,128)}, f32[32,34,1]{1,0,2:T(8,128)}, u32[]{:S(2)}, u32[]{:S(2)}) collective-permute-start(f32[32,34,1]{1,0,2:T(8,128)} %copy.133), channel_id=1, source_target_pairs={{1,0},{2,1},{3,2},{4,3},{5,4},{6,5},{7,6},{8,7},{9,8},{10,9},{11,1... | collective-permute-start | bytes 13064 | tf_op jit(solution)/shard_map/ppermute | solution.py:24
  144.7 2.1 fusion.4
  146.8 2.1 copy.106
  151.0 2.4 fusion.24
  155.4 3.4 %collective-permute-start.19 = (f32[32,1,256]{2,0,1:T(8,128)S(1)}, f32[32,1,256]{2,0,1:T(8,128)S(1)}, u32[]{:S(2)}, u32[]{:S(2)}) collective-permute-start(f32[32,1,256]{2,0,1:T(8,128)S(1)} %get-tuple-element.21), channel_id=1, source_target_pairs={{0,16},{16,32},{32,48},{48,64},{64,80},{80,96},{96,112},{112,128},... | collective-permute-start | bytes 98312 | tf_op jit(solution)/shard_map/ppermute | solution.py:23
  158.8 2.2 fusion.3
  161.0 3.0 collective-permute-done.19
  170.0 10.8 %collective-permute-start.20 = (f32[32,34,1]{1,0,2:T(8,128)}, f32[32,34,1]{1,0,2:T(8,128)}, u32[]{:S(2)}, u32[]{:S(2)}) collective-permute-start(f32[32,34,1]{1,0,2:T(8,128)} %copy.135), channel_id=1, source_target_pairs={{1,0},{2,1},{3,2},{4,3},{5,4},{6,5},{7,6},{8,7},{9,8},{10,9},{11,1... | collective-permute-start | bytes 13064 | tf_op jit(solution)/shard_map/ppermute | solution.py:24
  180.8 2.1 fusion.2
  182.9 2.2 copy.112
  185.1 2.1 copy.110
  191.0 7.5 %collective-permute-start.22 = (f32[32,1,256]{2,0,1:T(8,128)S(1)}, f32[32,1,256]{2,0,1:T(8,128)S(1)}, u32[]{:S(2)}, u32[]{:S(2)}) collective-permute-start(f32[32,1,256]{2,0,1:T(8,128)S(1)} %get-tuple-element.19), channel_id=1, source_target_pairs={{16,0},{32,16},{48,32},{64,48},{80,64},{96,80},{112,96},{128,112},... | collective-permute-start | bytes 98312 | tf_op jit(solution)/shard_map/ppermute | solution.py:24
  198.5 2.1 fusion.1
  200.7 2.2 fusion
  202.8 105.7 %psum.7 = f32[5,64,32]{2,1,0:T(8,128)S(1)} all-reduce(f32[5,64,32]{2,1,0:T(8,128)S(1)} %fusion), channel_id=1, replica_groups=mesh['sx'=32,'sy'=16] {'sx','sy'}, use_global_device_ids=true, to_apply=%region_0.1 | all-reduce | flops 10240 | bytes 81920 | tf_op jit(solution)/shard_map/psum | solution.py:95
  (135 shorter events, 55.3 us)
Async XLA Ops:
  0.0 144.7 %copy-start = (bf16[64,32,256]{2,1,0:T(8,128)(2,1)S(1)}, bf16[64,32,256]{2,1,0:T(8,128)(2,1)}, u32[]{:S(2)}) copy-start(bf16[64,32,256]{2,1,0:T(8,128)(2,1)} %param.7) | copy-start | bytes 3145732
  0.0 17.9 %copy-start.7 = (s32[2,32,256]{2,1,0:T(8,128)S(1)}, s32[2,32,256]{2,1,0:T(8,128)}, u32[]{:S(2)}) copy-start(s32[2,32,256]{2,1,0:T(8,128)} %param.10) | copy-start | bytes 196612
  1.5 29.1 %collective-permute-start = (f32[32,1,256]{2,0,1:T(8,128)S(1)}, f32[32,1,256]{2,0,1:T(8,128)S(1)}, u32[]{:S(2)}, u32[]{:S(2)}) collective-permute-start(f32[32,1,256]{2,0,1:T(8,128)S(1)} %get-tuple-element.30), channel_id=1, source_target_pairs={{16,0},{32,16},{48,32},{64,48},{80,64},{96,80},{112,96},{128,112},... | collective-permute-start | bytes 98312 | tf_op jit(solution)/shard_map/ppermute | solution.py:24
  16.0 14.6 %collective-permute-start.2 = (f32[32,1,256]{2,0,1:T(8,128)S(1)}, f32[32,1,256]{2,0,1:T(8,128)S(1)}, u32[]{:S(2)}, u32[]{:S(2)}) collective-permute-start(f32[32,1,256]{2,0,1:T(8,128)S(1)} %get-tuple-element.29), channel_id=1, source_target_pairs={{0,16},{16,32},{32,48},{48,64},{64,80},{80,96},{96,112},{112,128},... | collective-permute-start | bytes 98312 | tf_op jit(solution)/shard_map/ppermute | solution.py:23
  18.1 6.0 %collective-permute-start.4 = (s32[32,1]{0,1:T(1,128)S(1)}, s32[32,1]{0,1:T(1,128)S(1)}, u32[]{:S(2)}, u32[]{:S(2)}) collective-permute-start(s32[32,1]{0,1:T(1,128)S(1)} %bitcast.60), channel_id=1, source_target_pairs={{0,1},{1,2},{2,3},{3,4},{4,5},{5,6},{6,7},{7,8},{8,9},{9,10},{10,1... | collective-permute-start | bytes 392 | tf_op jit(solution)/shard_map/ppermute | solution.py:13
  22.1 8.5 %collective-permute-start.1 = (s32[1,256]{1,0:T(1,128)S(1)}, s32[1,256]{1,0:T(1,128)S(1)}, u32[]{:S(2)}, u32[]{:S(2)}) collective-permute-start(s32[1,256]{1,0:T(1,128)S(1)} %slice_bitcast_fusion.1), channel_id=1, source_target_pairs={{0,16},{16,32},{32,48},{48,64},{64,80},{80,96},{96,112},{112,128},... | collective-permute-start | bytes 3080 | tf_op jit(solution)/shard_map/ppermute | solution.py:13
  31.4 5.1 %collective-permute-start.5 = (f32[32,34,1]{1,0,2:T(8,128)S(1)}, f32[32,34,1]{1,0,2:T(8,128)S(1)}, u32[]{:S(2)}, u32[]{:S(2)}) collective-permute-start(f32[32,34,1]{1,0,2:T(8,128)S(1)} %copy.128), channel_id=1, source_target_pairs={{0,1},{1,2},{2,3},{3,4},{4,5},{5,6},{6,7},{7,8},{8,9},{9,10},{10,1... | collective-permute-start | bytes 13064 | tf_op jit(solution)/shard_map/ppermute | solution.py:23
  34.6 5.3 %collective-permute-start.3 = (f32[32,34,1]{1,0,2:T(8,128)S(1)}, f32[32,34,1]{1,0,2:T(8,128)S(1)}, u32[]{:S(2)}, u32[]{:S(2)}) collective-permute-start(f32[32,34,1]{1,0,2:T(8,128)S(1)} %copy.127), channel_id=1, source_target_pairs={{1,0},{2,1},{3,2},{4,3},{5,4},{6,5},{7,6},{8,7},{9,8},{10,9},{11,1... | collective-permute-start | bytes 13064 | tf_op jit(solution)/shard_map/ppermute | solution.py:24
  43.3 36.6 %copy-start.5 = (f32[32,32,256]{2,0,1:T(8,128)}, f32[32,32,256]{2,0,1:T(8,128)S(1)}, u32[]{:S(2)}) copy-start(f32[32,32,256]{2,0,1:T(8,128)S(1)} %fusion.44) | copy-start | bytes 3145732
  43.3 6.8 %collective-permute-start.6 = (f32[32,1,256]{2,0,1:T(8,128)S(1)}, f32[32,1,256]{2,0,1:T(8,128)S(1)}, u32[]{:S(2)}, u32[]{:S(2)}) collective-permute-start(f32[32,1,256]{2,0,1:T(8,128)S(1)} %get-tuple-element.28), channel_id=1, source_target_pairs={{16,0},{32,16},{48,32},{64,48},{80,64},{96,80},{112,96},{128,112},... | collective-permute-start | bytes 98312 | tf_op jit(solution)/shard_map/ppermute | solution.py:24
  47.5 8.6 %collective-permute-start.7 = (f32[32,1,256]{2,0,1:T(8,128)S(1)}, f32[32,1,256]{2,0,1:T(8,128)S(1)}, u32[]{:S(2)}, u32[]{:S(2)}) collective-permute-start(f32[32,1,256]{2,0,1:T(8,128)S(1)} %get-tuple-element.27), channel_id=1, source_target_pairs={{0,16},{16,32},{32,48},{48,64},{64,80},{80,96},{96,112},{112,128},... | collective-permute-start | bytes 98312 | tf_op jit(solution)/shard_map/ppermute | solution.py:23
  50.1 29.8 %copy-start.8 = (f32[32,1,256]{2,0,1:T(8,128)}, f32[32,1,256]{2,0,1:T(8,128)S(1)}, u32[]{:S(2)}) copy-start(f32[32,1,256]{2,0,1:T(8,128)S(1)} %collective-permute-done.6) | copy-start | bytes 98308
  56.0 23.9 %copy-start.10 = (f32[32,1,256]{2,0,1:T(8,128)}, f32[32,1,256]{2,0,1:T(8,128)S(1)}, u32[]{:S(2)}) copy-start(f32[32,1,256]{2,0,1:T(8,128)S(1)} %collective-permute-done.7) | copy-start | bytes 98308
  58.8 17.7 %collective-permute-start.9 = (f32[32,34,1]{1,0,2:T(8,128)S(1)}, f32[32,34,1]{1,0,2:T(8,128)S(1)}, u32[]{:S(2)}, u32[]{:S(2)}) collective-permute-start(f32[32,34,1]{1,0,2:T(8,128)S(1)} %copy.130), channel_id=1, source_target_pairs={{0,1},{1,2},{2,3},{3,4},{4,5},{5,6},{6,7},{7,8},{8,9},{9,10},{10,1... | collective-permute-start | bytes 13064 | tf_op jit(solution)/shard_map/ppermute | solution.py:23
  62.7 15.1 %collective-permute-start.8 = (f32[32,34,1]{1,0,2:T(8,128)S(1)}, f32[32,34,1]{1,0,2:T(8,128)}, u32[]{:S(2)}, u32[]{:S(2)}) collective-permute-start(f32[32,34,1]{1,0,2:T(8,128)S(1)} %copy.129), channel_id=1, source_target_pairs={{1,0},{2,1},{3,2},{4,3},{5,4},{6,5},{7,6},{8,7},{9,8},{10,9},{11,1... | collective-permute-start | bytes 13064 | tf_op jit(solution)/shard_map/ppermute | solution.py:24
  82.9 5.3 %collective-permute-start.10 = (f32[32,1,256]{2,0,1:T(8,128)S(1)}, f32[32,1,256]{2,0,1:T(8,128)S(1)}, u32[]{:S(2)}, u32[]{:S(2)}) collective-permute-start(f32[32,1,256]{2,0,1:T(8,128)S(1)} %get-tuple-element.26), channel_id=1, source_target_pairs={{16,0},{32,16},{48,32},{64,48},{80,64},{96,80},{112,96},{128,112},... | collective-permute-start | bytes 98312 | tf_op jit(solution)/shard_map/ppermute | solution.py:24
  84.8 8.6 %collective-permute-start.11 = (f32[32,1,256]{2,0,1:T(8,128)S(1)}, f32[32,1,256]{2,0,1:T(8,128)S(1)}, u32[]{:S(2)}, u32[]{:S(2)}) collective-permute-start(f32[32,1,256]{2,0,1:T(8,128)S(1)} %get-tuple-element.25), channel_id=1, source_target_pairs={{0,16},{16,32},{32,48},{48,64},{64,80},{80,96},{96,112},{112,128},... | collective-permute-start | bytes 98312 | tf_op jit(solution)/shard_map/ppermute | solution.py:23
  88.2 21.9 %copy-start.12 = (f32[32,1,256]{2,0,1:T(8,128)}, f32[32,1,256]{2,0,1:T(8,128)S(1)}, u32[]{:S(2)}) copy-start(f32[32,1,256]{2,0,1:T(8,128)S(1)} %collective-permute-done.10) | copy-start | bytes 98308
  93.4 16.7 %copy-start.14 = (f32[32,1,256]{2,0,1:T(8,128)}, f32[32,1,256]{2,0,1:T(8,128)S(1)}, u32[]{:S(2)}) copy-start(f32[32,1,256]{2,0,1:T(8,128)S(1)} %collective-permute-done.11) | copy-start | bytes 98308
  94.1 13.3 %collective-permute-start.13 = (f32[32,34,1]{1,0,2:T(8,128)S(1)}, f32[32,34,1]{1,0,2:T(8,128)S(1)}, u32[]{:S(2)}, u32[]{:S(2)}) collective-permute-start(f32[32,34,1]{1,0,2:T(8,128)S(1)} %copy.132), channel_id=1, source_target_pairs={{0,1},{1,2},{2,3},{3,4},{4,5},{5,6},{6,7},{7,8},{8,9},{9,10},{10,1... | collective-permute-start | bytes 13064 | tf_op jit(solution)/shard_map/ppermute | solution.py:23
  96.6 12.2 %collective-permute-start.12 = (f32[32,34,1]{1,0,2:T(8,128)S(1)}, f32[32,34,1]{1,0,2:T(8,128)S(1)}, u32[]{:S(2)}, u32[]{:S(2)}) collective-permute-start(f32[32,34,1]{1,0,2:T(8,128)S(1)} %copy.131), channel_id=1, source_target_pairs={{1,0},{2,1},{3,2},{4,3},{5,4},{6,5},{7,6},{8,7},{9,8},{10,9},{11,1... | collective-permute-start | bytes 13064 | tf_op jit(solution)/shard_map/ppermute | solution.py:24
  115.9 5.3 %collective-permute-start.14 = (f32[32,1,256]{2,0,1:T(8,128)S(1)}, f32[32,1,256]{2,0,1:T(8,128)S(1)}, u32[]{:S(2)}, u32[]{:S(2)}) collective-permute-start(f32[32,1,256]{2,0,1:T(8,128)S(1)} %get-tuple-element.24), channel_id=1, source_target_pairs={{16,0},{32,16},{48,32},{64,48},{80,64},{96,80},{112,96},{128,112},... | collective-permute-start | bytes 98312 | tf_op jit(solution)/shard_map/ppermute | solution.py:24
  117.8 8.6 %collective-permute-start.15 = (f32[32,1,256]{2,0,1:T(8,128)S(1)}, f32[32,1,256]{2,0,1:T(8,128)S(1)}, u32[]{:S(2)}, u32[]{:S(2)}) collective-permute-start(f32[32,1,256]{2,0,1:T(8,128)S(1)} %get-tuple-element.23), channel_id=1, source_target_pairs={{0,16},{16,32},{32,48},{48,64},{64,80},{80,96},{96,112},{112,128},... | collective-permute-start | bytes 98312 | tf_op jit(solution)/shard_map/ppermute | solution.py:23
  129.7 17.1 %collective-permute-start.17 = (f32[32,34,1]{1,0,2:T(8,128)S(1)}, f32[32,34,1]{1,0,2:T(8,128)}, u32[]{:S(2)}, u32[]{:S(2)}) collective-permute-start(f32[32,34,1]{1,0,2:T(8,128)S(1)} %copy.134), channel_id=1, source_target_pairs={{0,1},{1,2},{2,3},{3,4},{4,5},{5,6},{6,7},{7,8},{8,9},{9,10},{10,1... | collective-permute-start | bytes 13064 | tf_op jit(solution)/shard_map/ppermute | solution.py:23
  133.7 15.3 %collective-permute-start.16 = (f32[32,34,1]{1,0,2:T(8,128)}, f32[32,34,1]{1,0,2:T(8,128)}, u32[]{:S(2)}, u32[]{:S(2)}) collective-permute-start(f32[32,34,1]{1,0,2:T(8,128)} %copy.133), channel_id=1, source_target_pairs={{1,0},{2,1},{3,2},{4,3},{5,4},{6,5},{7,6},{8,7},{9,8},{10,9},{11,1... | collective-permute-start | bytes 13064 | tf_op jit(solution)/shard_map/ppermute | solution.py:24
  153.4 7.5 %collective-permute-start.18 = (f32[32,1,256]{2,0,1:T(8,128)S(1)}, f32[32,1,256]{2,0,1:T(8,128)S(1)}, u32[]{:S(2)}, u32[]{:S(2)}) collective-permute-start(f32[32,1,256]{2,0,1:T(8,128)S(1)} %get-tuple-element.22), channel_id=1, source_target_pairs={{16,0},{32,16},{48,32},{64,48},{80,64},{96,80},{112,96},{128,112},... | collective-permute-start | bytes 98312 | tf_op jit(solution)/shard_map/ppermute | solution.py:24
  155.4 8.6 %collective-permute-start.19 = (f32[32,1,256]{2,0,1:T(8,128)S(1)}, f32[32,1,256]{2,0,1:T(8,128)S(1)}, u32[]{:S(2)}, u32[]{:S(2)}) collective-permute-start(f32[32,1,256]{2,0,1:T(8,128)S(1)} %get-tuple-element.21), channel_id=1, source_target_pairs={{0,16},{16,32},{32,48},{48,64},{64,80},{80,96},{96,112},{112,128},... | collective-permute-start | bytes 98312 | tf_op jit(solution)/shard_map/ppermute | solution.py:23
  167.0 15.9 %collective-permute-start.21 = (f32[32,34,1]{1,0,2:T(8,128)S(1)}, f32[32,34,1]{1,0,2:T(8,128)}, u32[]{:S(2)}, u32[]{:S(2)}) collective-permute-start(f32[32,34,1]{1,0,2:T(8,128)S(1)} %copy.136), channel_id=1, source_target_pairs={{0,1},{1,2},{2,3},{3,4},{4,5},{5,6},{6,7},{7,8},{8,9},{9,10},{10,1... | collective-permute-start | bytes 13064 | tf_op jit(solution)/shard_map/ppermute | solution.py:23
  170.0 15.1 %collective-permute-start.20 = (f32[32,34,1]{1,0,2:T(8,128)}, f32[32,34,1]{1,0,2:T(8,128)}, u32[]{:S(2)}, u32[]{:S(2)}) collective-permute-start(f32[32,34,1]{1,0,2:T(8,128)} %copy.135), channel_id=1, source_target_pairs={{1,0},{2,1},{3,2},{4,3},{5,4},{6,5},{7,6},{8,7},{9,8},{10,9},{11,1... | collective-permute-start | bytes 13064 | tf_op jit(solution)/shard_map/ppermute | solution.py:24
  189.1 11.5 %collective-permute-start.23 = (f32[32,1,256]{2,0,1:T(8,128)S(1)}, f32[32,1,256]{2,0,1:T(8,128)S(1)}, u32[]{:S(2)}, u32[]{:S(2)}) collective-permute-start(f32[32,1,256]{2,0,1:T(8,128)S(1)} %get-tuple-element.20), channel_id=1, source_target_pairs={{0,16},{16,32},{32,48},{48,64},{64,80},{80,96},{96,112},{112,128},... | collective-permute-start | bytes 98312 | tf_op jit(solution)/shard_map/ppermute | solution.py:23
  191.0 9.6 %collective-permute-start.22 = (f32[32,1,256]{2,0,1:T(8,128)S(1)}, f32[32,1,256]{2,0,1:T(8,128)S(1)}, u32[]{:S(2)}, u32[]{:S(2)}) collective-permute-start(f32[32,1,256]{2,0,1:T(8,128)S(1)} %get-tuple-element.19), channel_id=1, source_target_pairs={{16,0},{32,16},{48,32},{64,48},{80,64},{96,80},{112,96},{128,112},... | collective-permute-start | bytes 98312 | tf_op jit(solution)/shard_map/ppermute | solution.py:24
  200.6 107.9 %copy-start.27 = (s32[5]{0:T(128)S(1)}, s32[5]{0:T(128)}, u32[]{:S(2)}) copy-start(s32[5]{0:T(128)} %param.11) | copy-start | bytes 64
  (20 other events, 186.7 us)
where the time goes:
time: 311 us; the launch traced here: 309 us
  starting transfers between devices  110 us (35%)
  blocking collectives  106 us (34%)
  local copies, waits for them, and re-layouts  34.3 us (11%)
  waiting for transfers between devices  27.7 us (9%)
  other arithmetic  20.3 us (7%)
  matrix products  10.8 us (3%)
    psum x1, blocking collectives, shards(): total = lax.psum(partial_tiles, ('sx', 'sy'))  106 us
    ppermute x11, starting transfers between devices, with_halo(): after = lax.ppermute(initial, axis, down)  76.9 us
    ppermute x11, starting transfers between devices, with_halo(): before = lax.ppermute(last, axis, up)  27 us
    ppermute x11, waiting for transfers between devices, with_halo(): before = lax.ppermute(last, axis, up)  19.3 us
    unnamed x66, local copies, waits for them, and re-layouts  11.6 us
    dot_general x5, matrix products, shards(): jnp.dot(left_flat, moved.T, precision=lax.Precision.HIGHEST, preferred_el...  10.6 us
    sub x3, other arithmetic, shards(): u_next = 2.0 * image - u_prev  10.2 us
    ppermute x5, local copies, waits for them, and re-layouts, with_halo(): after = lax.ppermute(initial, axis, down)  8.93 us
  transfers between devices with their start and end apart: 24, of which 6 were waited for; matrix products, arithmetic and copies ran while one was open for 9% of the time, Pallas kernels for 0%

commit v1 on v0

--- a/solution.py
+++ b/solution.py
@@ -2,6 +2,7 @@
 import jax.numpy as jnp
 from jax import lax
 from jax.sharding import PartitionSpec as P
+from jax.lax import psum
 
 MOMENTS = 5
 half_root = 0.8660254037844386
@@ -92,7 +93,7 @@
             u_prev, u_now = (u_now, u_next)
     partial_tiles = jnp.stack(moments)
     owned = nleft // lax.axis_size("sy")
-    total = lax.psum(partial_tiles, ("sx", "sy"))
+    total = psum(psum(partial_tiles, "sx"), "sy")
     mine = lax.dynamic_slice_in_dim(total, lax.axis_index("sy") * owned, owned, 1)
     all_sites = cells * lax.axis_size("sx") * lax.axis_size("sy")
     mine = mine * (1.0 / jnp.sqrt(jnp.float32(all_sites)))

time: 311 us -> 450 us (1.45)
  blocking collectives: 106 us -> 240 us
    psum x1 -> x2, blocking collectives: 106 us -> 240 us  [shards(): total = psum(psum(partial_tiles, 'sx'), 'sy')]
    unnamed x66 -> x62, local copies, waits for them, and re-layouts: 11.6 us -> 12.6 us
  transfers between devices with their start and end apart: 24 -> 24, of which waited for: 6 -> 6; matrix products, arithmetic and copies ran while one was open for 9% -> 6% of each run, Pallas kernels for 0% -> 0%
where the time goes in v1:
time: 450 us; the launch traced here: 444 us
  blocking collectives  240 us (53%)
  starting transfers between devices  110 us (24%)
  local copies, waits for them, and re-layouts  35.3 us (8%)
  waiting for transfers between devices  27.8 us (6%)
  other arithmetic  20.2 us (4%)
  matrix products  10.8 us (2%)
    psum x2, blocking collectives, shards(): total = psum(psum(partial_tiles, 'sx'), 'sy')  240 us
    ppermute x11, starting transfers between devices, with_halo(): after = lax.ppermute(initial, axis, down)  76.9 us
    ppermute x11, starting transfers between devices, with_halo(): before = lax.ppermute(last, axis, up)  27 us
    ppermute x11, waiting for transfers between devices, with_halo(): before = lax.ppermute(last, axis, up)  19.4 us
    unnamed x62, local copies, waits for them, and re-layouts  12.6 us
    dot_general x5, matrix products, shards(): jnp.dot(left_flat, moved.T, precision=lax.Precision.HIGHEST, preferred_el...  10.6 us
    sub x3, other arithmetic, shards(): u_next = 2.0 * image - u_prev  10.3 us
  transfers between devices with their start and end apart: 24, of which 6 were waited for; matrix products, arithmetic and copies ran while one was open for 6% of the time, Pallas kernels for 0%

profile of v1, /device:TPU:1, one launch (start us, length us, event | category | flops | bytes accessed | tf_op | source)
XLA Modules:
  0.0 444.4 jit_solution(15462017902587226464)
XLA Ops:
  1.5 14.5 %collective-permute-start = (f32[32,1,256]{2,0,1:T(8,128)S(1)}, f32[32,1,256]{2,0,1:T(8,128)S(1)}, u32[]{:S(2)}, u32[]{:S(2)}) collective-permute-start(f32[32,1,256]{2,0,1:T(8,128)S(1)} %get-tuple-element.30), channel_id=1, source_target_pairs={{16,0},{32,16},{48,32},{64,48},{80,64},{96,80},{112,96},{128,112},... | collective-permute-start | bytes 98312 | tf_op jit(solution)/shard_map/ppermute | solution.py:25
  18.1 4.0 collective-permute-start.4
  24.3 6.3 %collective-permute-done.1 = s32[1,256]{1,0:T(1,128)S(1)} collective-permute-done((s32[1,256]{1,0:T(1,128)S(1)}, s32[1,256]{1,0:T(1,128)S(1)}, u32[]{:S(2)}, u32[]{:S(2)}) %collective-permute-start.1) | collective-permute-done | bytes 1056 | tf_op jit(solution)/shard_map/ppermute | solution.py:14
  31.3 2.8 collective-permute-start.5
  43.2 4.2 collective-permute-start.6
  50.0 6.0 %collective-permute-done.7 = f32[32,1,256]{2,0,1:T(8,128)S(1)} collective-permute-done((f32[32,1,256]{2,0,1:T(8,128)S(1)}, f32[32,1,256]{2,0,1:T(8,128)S(1)}, u32[]{:S(2)}, u32[]{:S(2)}) %collective-permute-start.7) | collective-permute-done | bytes 32800 | tf_op jit(solution)/shard_map/ppermute | solution.py:24
  58.7 2.6 collective-permute-start.9
  62.7 10.5 %collective-permute-start.8 = (f32[32,34,1]{1,0,2:T(8,128)S(1)}, f32[32,34,1]{1,0,2:T(8,128)}, u32[]{:S(2)}, u32[]{:S(2)}) collective-permute-start(f32[32,34,1]{1,0,2:T(8,128)S(1)} %copy.129), channel_id=1, source_target_pairs={{1,0},{2,1},{3,2},{4,3},{5,4},{6,5},{7,6},{8,7},{9,8},{10,9},{11,1... | collective-permute-start | bytes 13064 | tf_op jit(solution)/shard_map/ppermute | solution.py:25
  73.2 3.1 broadcast_multiply_fusion.1
  77.6 2.1 copy.92
  79.7 2.9 broadcast_multiply_fusion
  84.6 3.4 collective-permute-start.11
  87.9 5.2 %collective-permute-done.11 = f32[32,1,256]{2,0,1:T(8,128)S(1)} collective-permute-done((f32[32,1,256]{2,0,1:T(8,128)S(1)}, f32[32,1,256]{2,0,1:T(8,128)S(1)}, u32[]{:S(2)}, u32[]{:S(2)}) %collective-permute-start.11) | collective-permute-done | bytes 32800 | tf_op jit(solution)/shard_map/ppermute | solution.py:24
  96.3 10.8 %collective-permute-start.12 = (f32[32,34,1]{1,0,2:T(8,128)S(1)}, f32[32,34,1]{1,0,2:T(8,128)S(1)}, u32[]{:S(2)}, u32[]{:S(2)}) collective-permute-start(f32[32,34,1]{1,0,2:T(8,128)S(1)} %copy.131), channel_id=1, source_target_pairs={{1,0},{2,1},{3,2},{4,3},{5,4},{6,5},{7,6},{8,7},{9,8},{10,9},{11,1... | collective-permute-start | bytes 13064 | tf_op jit(solution)/shard_map/ppermute | solution.py:25
  109.9 6.0 %fusion.32 = f32[32,32,256]{2,0,1:T(8,128)S(1)} fusion(f32[32,34,1]{2,0,1:T(8,128)} %copy.100, f32[32,1,256]{2,0,1:T(8,128)S(1)} %collective-permute-done.10, f32[32,32,256]{2,0,1:T(8,128)} %copy-done.1, f32[32,1,256]{2,0,1:T(8,128)S(1)} %collective-permute-done.11, f32[32,34,1]{2,0,1:T(8,128)} %copy.98, f32[32,32,256]{2,0,1:T(8,128)} %get-tuple-element.8, ...), kind=kLoop, calls=%fused_computation.59 | loop fusion | flops 9175040 | bytes 4539392 | tf_op jit(solution)/shard_map/sub | solution.py:92
  117.8 3.4 collective-permute-start.15
  121.2 5.2 %collective-permute-done.15 = f32[32,1,256]{2,0,1:T(8,128)S(1)} collective-permute-done((f32[32,1,256]{2,0,1:T(8,128)S(1)}, f32[32,1,256]{2,0,1:T(8,128)S(1)}, u32[]{:S(2)}, u32[]{:S(2)}) %collective-permute-start.15) | collective-permute-done | bytes 32800 | tf_op jit(solution)/shard_map/ppermute | solution.py:24
  133.6 11.0 %collective-permute-start.16 = (f32[32,34,1]{1,0,2:T(8,128)}, f32[32,34,1]{1,0,2:T(8,128)}, u32[]{:S(2)}, u32[]{:S(2)}) collective-permute-start(f32[32,34,1]{1,0,2:T(8,128)} %copy.133), channel_id=1, source_target_pairs={{1,0},{2,1},{3,2},{4,3},{5,4},{6,5},{7,6},{8,7},{9,8},{10,9},{11,1... | collective-permute-start | bytes 13064 | tf_op jit(solution)/shard_map/ppermute | solution.py:25
  144.6 2.1 fusion.4
  146.8 2.1 copy.106
  150.9 2.4 fusion.24
  155.3 3.4 collective-permute-start.19
  158.7 2.2 fusion.3
  160.9 3.0 collective-permute-done.19
  171.0 10.8 %collective-permute-start.20 = (f32[32,34,1]{1,0,2:T(8,128)}, f32[32,34,1]{1,0,2:T(8,128)}, u32[]{:S(2)}, u32[]{:S(2)}) collective-permute-start(f32[32,34,1]{1,0,2:T(8,128)} %copy.135), channel_id=1, source_target_pairs={{1,0},{2,1},{3,2},{4,3},{5,4},{6,5},{7,6},{8,7},{9,8},{10,9},{11,1... | collective-permute-start | bytes 13064 | tf_op jit(solution)/shard_map/ppermute | solution.py:25
  181.9 2.1 fusion.2
  184.0 2.1 copy.112
  192.0 7.5 %collective-permute-start.22 = (f32[32,1,256]{2,0,1:T(8,128)S(1)}, f32[32,1,256]{2,0,1:T(8,128)S(1)}, u32[]{:S(2)}, u32[]{:S(2)}) collective-permute-start(f32[32,1,256]{2,0,1:T(8,128)S(1)} %get-tuple-element.19), channel_id=1, source_target_pairs={{16,0},{32,16},{48,32},{64,48},{80,64},{96,80},{112,96},{128,112},... | collective-permute-start | bytes 98312 | tf_op jit(solution)/shard_map/ppermute | solution.py:25
  199.5 2.1 fusion.1
  201.7 2.2 fusion
  203.8 125.3 %psum.14 = f32[5,64,32]{2,1,0:T(8,128)S(1)} all-reduce(f32[5,64,32]{2,1,0:T(8,128)S(1)} %fusion), channel_id=1, replica_groups=mesh['sx'=32,'sy'=16] {'sx'}, use_global_device_ids=true, to_apply=%region_0.1 | all-reduce | flops 10240 | bytes 81920 | tf_op jit(solution)/shard_map/psum | solution.py:96
  329.1 114.4 %psum.15 = f32[5,64,32]{2,1,0:T(8,128)S(1)} all-reduce(f32[5,64,32]{2,1,0:T(8,128)S(1)} %psum.14), channel_id=1, replica_groups=mesh['sx'=32,'sy'=16] {'sy'}, use_global_device_ids=true, to_apply=%region_1.2 | all-reduce | flops 10240 | bytes 81920 | tf_op jit(solution)/shard_map/psum | solution.py:96
  (132 shorter events, 58.4 us)
Async XLA Ops:
  0.0 144.6 %copy-start = (bf16[64,32,256]{2,1,0:T(8,128)(2,1)S(1)}, bf16[64,32,256]{2,1,0:T(8,128)(2,1)}, u32[]{:S(2)}) copy-start(bf16[64,32,256]{2,1,0:T(8,128)(2,1)} %param.7) | copy-start | bytes 3145732
  0.0 17.9 %copy-start.5 = (s32[2,32,256]{2,1,0:T(8,128)S(1)}, s32[2,32,256]{2,1,0:T(8,128)}, u32[]{:S(2)}) copy-start(s32[2,32,256]{2,1,0:T(8,128)} %param.10) | copy-start | bytes 196612
  1.5 29.1 %collective-permute-start = (f32[32,1,256]{2,0,1:T(8,128)S(1)}, f32[32,1,256]{2,0,1:T(8,128)S(1)}, u32[]{:S(2)}, u32[]{:S(2)}) collective-permute-start(f32[32,1,256]{2,0,1:T(8,128)S(1)} %get-tuple-element.30), channel_id=1, source_target_pairs={{16,0},{32,16},{48,32},{64,48},{80,64},{96,80},{112,96},{128,112},... | collective-permute-start | bytes 98312 | tf_op jit(solution)/shard_map/ppermute | solution.py:25
  16.0 14.6 %collective-permute-start.2 = (f32[32,1,256]{2,0,1:T(8,128)S(1)}, f32[32,1,256]{2,0,1:T(8,128)S(1)}, u32[]{:S(2)}, u32[]{:S(2)}) collective-permute-start(f32[32,1,256]{2,0,1:T(8,128)S(1)} %get-tuple-element.29), channel_id=1, source_target_pairs={{0,16},{16,32},{32,48},{48,64},{64,80},{80,96},{96,112},{112,128},... | collective-permute-start | bytes 98312 | tf_op jit(solution)/shard_map/ppermute | solution.py:24
  18.1 6.0 %collective-permute-start.4 = (s32[32,1]{0,1:T(1,128)S(1)}, s32[32,1]{0,1:T(1,128)S(1)}, u32[]{:S(2)}, u32[]{:S(2)}) collective-permute-start(s32[32,1]{0,1:T(1,128)S(1)} %bitcast.60), channel_id=1, source_target_pairs={{0,1},{1,2},{2,3},{3,4},{4,5},{5,6},{6,7},{7,8},{8,9},{9,10},{10,1... | collective-permute-start | bytes 392 | tf_op jit(solution)/shard_map/ppermute | solution.py:14
  22.1 8.5 %collective-permute-start.1 = (s32[1,256]{1,0:T(1,128)S(1)}, s32[1,256]{1,0:T(1,128)S(1)}, u32[]{:S(2)}, u32[]{:S(2)}) collective-permute-start(s32[1,256]{1,0:T(1,128)S(1)} %slice_bitcast_fusion.1), channel_id=1, source_target_pairs={{0,16},{16,32},{32,48},{48,64},{64,80},{80,96},{96,112},{112,128},... | collective-permute-start | bytes 3080 | tf_op jit(solution)/shard_map/ppermute | solution.py:14
  31.3 5.1 %collective-permute-start.5 = (f32[32,34,1]{1,0,2:T(8,128)S(1)}, f32[32,34,1]{1,0,2:T(8,128)S(1)}, u32[]{:S(2)}, u32[]{:S(2)}) collective-permute-start(f32[32,34,1]{1,0,2:T(8,128)S(1)} %copy.128), channel_id=1, source_target_pairs={{0,1},{1,2},{2,3},{3,4},{4,5},{5,6},{6,7},{7,8},{8,9},{9,10},{10,1... | collective-permute-start | bytes 13064 | tf_op jit(solution)/shard_map/ppermute | solution.py:24
  34.6 5.3 %collective-permute-start.3 = (f32[32,34,1]{1,0,2:T(8,128)S(1)}, f32[32,34,1]{1,0,2:T(8,128)S(1)}, u32[]{:S(2)}, u32[]{:S(2)}) collective-permute-start(f32[32,34,1]{1,0,2:T(8,128)S(1)} %copy.127), channel_id=1, source_target_pairs={{1,0},{2,1},{3,2},{4,3},{5,4},{6,5},{7,6},{8,7},{9,8},{10,9},{11,1... | collective-permute-start | bytes 13064 | tf_op jit(solution)/shard_map/ppermute | solution.py:25
  43.2 36.5 %copy-start.3 = (f32[32,32,256]{2,0,1:T(8,128)}, f32[32,32,256]{2,0,1:T(8,128)S(1)}, u32[]{:S(2)}) copy-start(f32[32,32,256]{2,0,1:T(8,128)S(1)} %fusion.44) | copy-start | bytes 3145732
  43.2 6.7 %collective-permute-start.6 = (f32[32,1,256]{2,0,1:T(8,128)S(1)}, f32[32,1,256]{2,0,1:T(8,128)S(1)}, u32[]{:S(2)}, u32[]{:S(2)}) collective-permute-start(f32[32,1,256]{2,0,1:T(8,128)S(1)} %get-tuple-element.28), channel_id=1, source_target_pairs={{16,0},{32,16},{48,32},{64,48},{80,64},{96,80},{112,96},{128,112},... | collective-permute-start | bytes 98312 | tf_op jit(solution)/shard_map/ppermute | solution.py:25
  47.4 8.6 %collective-permute-start.7 = (f32[32,1,256]{2,0,1:T(8,128)S(1)}, f32[32,1,256]{2,0,1:T(8,128)S(1)}, u32[]{:S(2)}, u32[]{:S(2)}) collective-permute-start(f32[32,1,256]{2,0,1:T(8,128)S(1)} %get-tuple-element.27), channel_id=1, source_target_pairs={{0,16},{16,32},{32,48},{48,64},{64,80},{80,96},{96,112},{112,128},... | collective-permute-start | bytes 98312 | tf_op jit(solution)/shard_map/ppermute | solution.py:24
  50.0 29.7 %copy-start.6 = (f32[32,1,256]{2,0,1:T(8,128)}, f32[32,1,256]{2,0,1:T(8,128)S(1)}, u32[]{:S(2)}) copy-start(f32[32,1,256]{2,0,1:T(8,128)S(1)} %collective-permute-done.6) | copy-start | bytes 98308
  56.0 23.7 %copy-start.8 = (f32[32,1,256]{2,0,1:T(8,128)}, f32[32,1,256]{2,0,1:T(8,128)S(1)}, u32[]{:S(2)}) copy-start(f32[32,1,256]{2,0,1:T(8,128)S(1)} %collective-permute-done.7) | copy-start | bytes 98308
  58.7 17.6 %collective-permute-start.9 = (f32[32,34,1]{1,0,2:T(8,128)S(1)}, f32[32,34,1]{1,0,2:T(8,128)S(1)}, u32[]{:S(2)}, u32[]{:S(2)}) collective-permute-start(f32[32,34,1]{1,0,2:T(8,128)S(1)} %copy.130), channel_id=1, source_target_pairs={{0,1},{1,2},{2,3},{3,4},{4,5},{5,6},{6,7},{7,8},{8,9},{9,10},{10,1... | collective-permute-start | bytes 13064 | tf_op jit(solution)/shard_map/ppermute | solution.py:24
  62.7 14.9 %collective-permute-start.8 = (f32[32,34,1]{1,0,2:T(8,128)S(1)}, f32[32,34,1]{1,0,2:T(8,128)}, u32[]{:S(2)}, u32[]{:S(2)}) collective-permute-start(f32[32,34,1]{1,0,2:T(8,128)S(1)} %copy.129), channel_id=1, source_target_pairs={{1,0},{2,1},{3,2},{4,3},{5,4},{6,5},{7,6},{8,7},{9,8},{10,9},{11,1... | collective-permute-start | bytes 13064 | tf_op jit(solution)/shard_map/ppermute | solution.py:25
  82.6 5.3 %collective-permute-start.10 = (f32[32,1,256]{2,0,1:T(8,128)S(1)}, f32[32,1,256]{2,0,1:T(8,128)S(1)}, u32[]{:S(2)}, u32[]{:S(2)}) collective-permute-start(f32[32,1,256]{2,0,1:T(8,128)S(1)} %get-tuple-element.26), channel_id=1, source_target_pairs={{16,0},{32,16},{48,32},{64,48},{80,64},{96,80},{112,96},{128,112},... | collective-permute-start | bytes 98312 | tf_op jit(solution)/shard_map/ppermute | solution.py:25
  84.6 8.6 %collective-permute-start.11 = (f32[32,1,256]{2,0,1:T(8,128)S(1)}, f32[32,1,256]{2,0,1:T(8,128)S(1)}, u32[]{:S(2)}, u32[]{:S(2)}) collective-permute-start(f32[32,1,256]{2,0,1:T(8,128)S(1)} %get-tuple-element.25), channel_id=1, source_target_pairs={{0,16},{16,32},{32,48},{48,64},{64,80},{80,96},{96,112},{112,128},... | collective-permute-start | bytes 98312 | tf_op jit(solution)/shard_map/ppermute | solution.py:24
  87.9 21.9 %copy-start.10 = (f32[32,1,256]{2,0,1:T(8,128)}, f32[32,1,256]{2,0,1:T(8,128)S(1)}, u32[]{:S(2)}) copy-start(f32[32,1,256]{2,0,1:T(8,128)S(1)} %collective-permute-done.10) | copy-start | bytes 98308
  93.1 16.8 %copy-start.12 = (f32[32,1,256]{2,0,1:T(8,128)}, f32[32,1,256]{2,0,1:T(8,128)S(1)}, u32[]{:S(2)}) copy-start(f32[32,1,256]{2,0,1:T(8,128)S(1)} %collective-permute-done.11) | copy-start | bytes 98308
  93.9 13.3 %collective-permute-start.13 = (f32[32,34,1]{1,0,2:T(8,128)S(1)}, f32[32,34,1]{1,0,2:T(8,128)S(1)}, u32[]{:S(2)}, u32[]{:S(2)}) collective-permute-start(f32[32,34,1]{1,0,2:T(8,128)S(1)} %copy.132), channel_id=1, source_target_pairs={{0,1},{1,2},{2,3},{3,4},{4,5},{5,6},{6,7},{7,8},{8,9},{9,10},{10,1... | collective-permute-start | bytes 13064 | tf_op jit(solution)/shard_map/ppermute | solution.py:24
  96.3 12.2 %collective-permute-start.12 = (f32[32,34,1]{1,0,2:T(8,128)S(1)}, f32[32,34,1]{1,0,2:T(8,128)S(1)}, u32[]{:S(2)}, u32[]{:S(2)}) collective-permute-start(f32[32,34,1]{1,0,2:T(8,128)S(1)} %copy.131), channel_id=1, source_target_pairs={{1,0},{2,1},{3,2},{4,3},{5,4},{6,5},{7,6},{8,7},{9,8},{10,9},{11,1... | collective-permute-start | bytes 13064 | tf_op jit(solution)/shard_map/ppermute | solution.py:25
  115.9 5.3 %collective-permute-start.14 = (f32[32,1,256]{2,0,1:T(8,128)S(1)}, f32[32,1,256]{2,0,1:T(8,128)S(1)}, u32[]{:S(2)}, u32[]{:S(2)}) collective-permute-start(f32[32,1,256]{2,0,1:T(8,128)S(1)} %get-tuple-element.24), channel_id=1, source_target_pairs={{16,0},{32,16},{48,32},{64,48},{80,64},{96,80},{112,96},{128,112},... | collective-permute-start | bytes 98312 | tf_op jit(solution)/shard_map/ppermute | solution.py:25
  117.8 8.6 %collective-permute-start.15 = (f32[32,1,256]{2,0,1:T(8,128)S(1)}, f32[32,1,256]{2,0,1:T(8,128)S(1)}, u32[]{:S(2)}, u32[]{:S(2)}) collective-permute-start(f32[32,1,256]{2,0,1:T(8,128)S(1)} %get-tuple-element.23), channel_id=1, source_target_pairs={{0,16},{16,32},{32,48},{48,64},{64,80},{80,96},{96,112},{112,128},... | collective-permute-start | bytes 98312 | tf_op jit(solution)/shard_map/ppermute | solution.py:24
  129.6 17.1 %collective-permute-start.17 = (f32[32,34,1]{1,0,2:T(8,128)S(1)}, f32[32,34,1]{1,0,2:T(8,128)}, u32[]{:S(2)}, u32[]{:S(2)}) collective-permute-start(f32[32,34,1]{1,0,2:T(8,128)S(1)} %copy.134), channel_id=1, source_target_pairs={{0,1},{1,2},{2,3},{3,4},{4,5},{5,6},{6,7},{7,8},{8,9},{9,10},{10,1... | collective-permute-start | bytes 13064 | tf_op jit(solution)/shard_map/ppermute | solution.py:24
  133.6 15.3 %collective-permute-start.16 = (f32[32,34,1]{1,0,2:T(8,128)}, f32[32,34,1]{1,0,2:T(8,128)}, u32[]{:S(2)}, u32[]{:S(2)}) collective-permute-start(f32[32,34,1]{1,0,2:T(8,128)} %copy.133), channel_id=1, source_target_pairs={{1,0},{2,1},{3,2},{4,3},{5,4},{6,5},{7,6},{8,7},{9,8},{10,9},{11,1... | collective-permute-start | bytes 13064 | tf_op jit(solution)/shard_map/ppermute | solution.py:25
  153.3 7.5 %collective-permute-start.18 = (f32[32,1,256]{2,0,1:T(8,128)S(1)}, f32[32,1,256]{2,0,1:T(8,128)S(1)}, u32[]{:S(2)}, u32[]{:S(2)}) collective-permute-start(f32[32,1,256]{2,0,1:T(8,128)S(1)} %get-tuple-element.22), channel_id=1, source_target_pairs={{16,0},{32,16},{48,32},{64,48},{80,64},{96,80},{112,96},{128,112},... | collective-permute-start | bytes 98312 | tf_op jit(solution)/shard_map/ppermute | solution.py:25
  155.3 8.6 %collective-permute-start.19 = (f32[32,1,256]{2,0,1:T(8,128)S(1)}, f32[32,1,256]{2,0,1:T(8,128)S(1)}, u32[]{:S(2)}, u32[]{:S(2)}) collective-permute-start(f32[32,1,256]{2,0,1:T(8,128)S(1)} %get-tuple-element.21), channel_id=1, source_target_pairs={{0,16},{16,32},{32,48},{48,64},{64,80},{80,96},{96,112},{112,128},... | collective-permute-start | bytes 98312 | tf_op jit(solution)/shard_map/ppermute | solution.py:24
  167.1 16.9 %collective-permute-start.21 = (f32[32,34,1]{1,0,2:T(8,128)S(1)}, f32[32,34,1]{1,0,2:T(8,128)}, u32[]{:S(2)}, u32[]{:S(2)}) collective-permute-start(f32[32,34,1]{1,0,2:T(8,128)S(1)} %copy.136), channel_id=1, source_target_pairs={{0,1},{1,2},{2,3},{3,4},{4,5},{5,6},{6,7},{7,8},{8,9},{9,10},{10,1... | collective-permute-start | bytes 13064 | tf_op jit(solution)/shard_map/ppermute | solution.py:24
  171.0 15.0 %collective-permute-start.20 = (f32[32,34,1]{1,0,2:T(8,128)}, f32[32,34,1]{1,0,2:T(8,128)}, u32[]{:S(2)}, u32[]{:S(2)}) collective-permute-start(f32[32,34,1]{1,0,2:T(8,128)} %copy.135), channel_id=1, source_target_pairs={{1,0},{2,1},{3,2},{4,3},{5,4},{6,5},{7,6},{8,7},{9,8},{10,9},{11,1... | collective-permute-start | bytes 13064 | tf_op jit(solution)/shard_map/ppermute | solution.py:25
  190.1 11.5 %collective-permute-start.23 = (f32[32,1,256]{2,0,1:T(8,128)S(1)}, f32[32,1,256]{2,0,1:T(8,128)S(1)}, u32[]{:S(2)}, u32[]{:S(2)}) collective-permute-start(f32[32,1,256]{2,0,1:T(8,128)S(1)} %get-tuple-element.20), channel_id=1, source_target_pairs={{0,16},{16,32},{32,48},{48,64},{64,80},{80,96},{96,112},{112,128},... | collective-permute-start | bytes 98312 | tf_op jit(solution)/shard_map/ppermute | solution.py:24
  192.0 9.6 %collective-permute-start.22 = (f32[32,1,256]{2,0,1:T(8,128)S(1)}, f32[32,1,256]{2,0,1:T(8,128)S(1)}, u32[]{:S(2)}, u32[]{:S(2)}) collective-permute-start(f32[32,1,256]{2,0,1:T(8,128)S(1)} %get-tuple-element.19), channel_id=1, source_target_pairs={{16,0},{32,16},{48,32},{64,48},{80,64},{96,80},{112,96},{128,112},... | collective-permute-start | bytes 98312 | tf_op jit(solution)/shard_map/ppermute | solution.py:25
  201.6 241.9 %copy-start.25 = (s32[5]{0:T(128)S(1)}, s32[5]{0:T(128)}, u32[]{:S(2)}) copy-start(s32[5]{0:T(128)} %param.11) | copy-start | bytes 64
  (18 other events, 173.7 us)
